TPU v7x, 32 devices: a whole 2x2x4 slice. The times are simulated.
32 devices in a mesh: blk: 8 (over y, x, core), slab: 4 (over z).
Axes of the slice: x: 2, y: 2, z: 4, core: 2. Of those that a mesh axis runs over, the one named last changes fastest.
Arguments:
- old_factor: bfloat16 [8192, 24576], P('slab', 'blk'), may hold values from -0.0546875 to 0.0546875
- solved: bfloat16 [24576, 256], P('blk', 'slab'), may hold values from -6 to 6
- band: bfloat16 [8192, 8192], P('blk'), may hold values from -0.0625 to 0.0625
- inv_diag: bfloat16 [2048, 8192], P(None, 'blk'), may hold values from -1 to 2, as said below
- rhs: bfloat16 [8192, 256], P('blk', 'slab'), may hold values from -6 to 6
Outputs:
- solution: bfloat16 [8192, 256], P('blk', 'slab')
Inputs may be any that keep to these rules, and one draw needn't show every extreme that they name: `inv_diag`: columns k * 2048 to (k + 1) * 2048 - 1 hold the inverse applied in block step k.
All inputs are finite; a program needn't handle non-finite values.
Results may differ from a plain program's by a relative error of at most 0.008.
Values may be sent and summed in bfloat16 or wider, within the bound.
A program may use at most 64 MiB of HBM per device.

v0:
```python
import jax
import jax.numpy as jnp
from jax import lax
from jax.sharding import PartitionSpec as P

STEPS = 4


def body(old_factor, solved, band, inv_diag, rhs):
    own_rows = rhs.shape[0]
    block_rows = inv_diag.shape[0]
    group_size = block_rows // own_rows
    own_index = lax.axis_index("blk")
    own_block = own_index // group_size
    offset = own_index % group_size * own_rows
    partial_value = jnp.dot(
        old_factor,
        lax.all_gather(solved, "slab", axis=1, tiled=True),
        preferred_element_type=jnp.float32,
    )
    window_terms = lax.all_to_all(partial_value, "slab", split_axis=1, concat_axis=0, tiled=True)
    source = rhs.astype(jnp.float32)
    accum = lax.psum_scatter(window_terms, "blk", scatter_dimension=0, tiled=True)
    solution = jnp.zeros(rhs.shape, jnp.bfloat16)
    for step in range(STEPS):
        total = accum
        resid = (source - total).astype(jnp.bfloat16)
        term = jnp.dot(inv_diag, resid, preferred_element_type=jnp.float32)
        term = jnp.where(own_block == step, term, jnp.zeros_like(term))
        newest = lax.psum(term, "blk").astype(jnp.bfloat16)
        mine = lax.dynamic_slice_in_dim(newest, offset, own_rows, 0)
        solution = jnp.where(own_block == step, mine, solution)
        if step + 1 < STEPS:
            columns = band[:, step * block_rows : (step + 1) * block_rows]
            update = jnp.dot(columns, newest, preferred_element_type=jnp.float32)
            accum = accum + jnp.where(own_block > step, update, jnp.zeros_like(update))
    return solution


def solution(mesh):
    return jax.shard_map(
        body,
        mesh=mesh,
        in_specs=(
            P("slab", "blk"),
            P("blk", "slab"),
            P("blk", None),
            P(None, "blk"),
            P("blk", "slab"),
        ),
        out_specs=P("blk", "slab"),
        check_vma=False,
    )
```

profile of v0, /device:TPU:31, one launch (start us, length us, event | category | flops | bytes accessed | tf_op | source)
XLA Modules:
  0.0 288.6 jit_solution(17000383142873836997)
XLA Ops:
  6.5 0.0 all-gather.2.cloned.1.call-start
  6.5 0.7 all-gather.2.cloned.1.call-update
  7.3 0.0 reduce-scatter.2.cloned.1.call-start
  7.3 37.6 %all-gather.2.cloned.1.call-done = bf16[3072,256]{0,1:T(8,128)(2,1)} async-done(((bf16[3072,64]{0,1:T(8,128)(2,1)}), bf16[3072,256]{0,1:T(8,128)(2,1)}) %all-gather.2.cloned.1.call-update) | async-done | bytes 1572880 | tf_op jit(solution)/shard_map/all_gather | solution.py:18
  44.9 6.9 %fusion.56 = f32[2048,256]{0,1:T(8,128)S(1)} fusion(bf16[2048,3072]{1,0:T(8,128)(2,1)} %param.5, bf16[3072,256]{0,1:T(8,128)(2,1)} %all-gather.2.cloned.1.call-done), kind=kOutput, calls=%fused_computation.37 | convolution fusion | flops 3221225472 | bytes 16252928 | tf_op jit(solution)/shard_map/dot_general | solution.py:16
  51.8 50.4 %all_to_all.19 = f32[2048,4,64]{0,2,1:T(8,128)S(1)} all-to-all(f32[2048,4,64]{0,2,1:T(8,128)S(1)} %bitcast.41), channel_id=1, replica_groups=mesh['blk'=8,'slab'=4] {'slab'}, dimensions={1} | all-to-all | bytes 4194304 | tf_op jit(solution)/shard_map/all_to_all | solution.py:21
  102.2 0.0 copy-start.2
  102.2 1.5 copy.7
  103.7 0.0 reduce-scatter.2.cloned.1.call-update
  103.8 41.5 %reduce-scatter.2.cloned.1.call-done = f32[1024,64]{0,1:T(8,128)} async-done(((f32[8192,64]{0,1:T(8,128)}), f32[1024,64]{0,1:T(8,128)}) %reduce-scatter.2.cloned.1.call-update) | async-done | bytes 262160 | tf_op jit(solution)/shard_map/reduce_scatter | solution.py:23
  145.3 0.0 copy-done.2
  145.3 0.0 copy-start.3
  145.3 3.7 %fusion.6 = f32[2048,64]{0,1:T(8,128)S(1)} fusion(bf16[2048,1024]{1,0:T(8,128)(2,1)} %param.8, pred[]{:T(512)S(6)} %eq.19, f32[1024,64]{0,1:T(8,128)} %reduce-scatter.2.cloned.1.call-done, bf16[1024,64]{0,1:T(8,128)(2,1)S(1)} %copy-done.2), kind=kOutput, calls=%fused_computation.10 | convolution fusion | flops 268763136 | bytes 5111809 | tf_op jit(solution)/shard_map/dot_general | solution.py:28
  149.0 29.0 %all-reduce.4 = bf16[2048,64]{0,1:T(8,128)(2,1)S(1)} all-reduce(f32[2048,64]{0,1:T(8,128)S(1)} %fusion.6), channel_id=1, replica_groups=mesh['blk'=8,'slab'=4] {'blk'}, use_global_device_ids=true, to_apply=%region_1.2 | all-reduce | flops 131072 | bytes 786432 | tf_op jit(solution)/shard_map/psum | solution.py:30
  178.0 0.0 copy-done.3
  178.0 0.0 copy-start
  178.0 3.7 %fusion.16 = f32[1024,64]{0,1:T(8,128)S(1)} fusion(f32[1024,64]{0,1:T(8,128)S(1)} %copy-done.3, bf16[2048,64]{0,1:T(8,128)(2,1)S(1)} %all-reduce.4, bf16[1024,8192]{1,0:T(8,128)(2,1)} %param.7, pred[]{:T(512)S(6)} %gt.9), kind=kOutput, calls=%fused_computation.16 | convolution fusion | flops 268566528 | bytes 4980737 | tf_op jit(solution)/shard_map/dot_general | solution.py:35
  181.7 0.0 copy-done
  181.7 1.4 fusion.7
  183.1 29.0 %all-reduce.5 = bf16[2048,64]{0,1:T(8,128)(2,1)S(1)} all-reduce(f32[2048,64]{0,1:T(8,128)S(1)} %fusion.7), channel_id=1, replica_groups=mesh['blk'=8,'slab'=4] {'blk'}, use_global_device_ids=true, to_apply=%region_2.3 | all-reduce | flops 131072 | bytes 786432 | tf_op jit(solution)/shard_map/psum | solution.py:30
  212.2 0.0 copy-start.1
  212.2 3.7 %fusion.25 = f32[1024,64]{0,1:T(8,128)S(1)} fusion(f32[1024,64]{0,1:T(8,128)S(1)} %fusion.16, bf16[2048,64]{0,1:T(8,128)(2,1)S(1)} %all-reduce.5, bf16[1024,8192]{1,0:T(8,128)(2,1)} %param.7, pred[]{:T(512)S(6)} %gt.10), kind=kOutput, calls=%fused_computation.19 | convolution fusion | flops 268566528 | bytes 4980737 | tf_op jit(solution)/shard_map/dot_general | solution.py:35
  215.9 0.0 copy-done.1
  215.9 1.4 fusion.8
  217.3 28.8 %all-reduce.6 = bf16[2048,64]{0,1:T(8,128)(2,1)S(1)} all-reduce(f32[2048,64]{0,1:T(8,128)S(1)} %fusion.8), channel_id=1, replica_groups=mesh['blk'=8,'slab'=4] {'blk'}, use_global_device_ids=true, to_apply=%region_3.4 | all-reduce | flops 131072 | bytes 786432 | tf_op jit(solution)/shard_map/psum | solution.py:30
  246.1 6.2 %fusion.9 = f32[2048,64]{0,1:T(8,128)S(1)} fusion(bf16[2048,1024]{1,0:T(8,128)(2,1)} %param.8, f32[1024,64]{0,1:T(8,128)S(1)} %fusion.25, bf16[2048,64]{0,1:T(8,128)(2,1)S(1)} %all-reduce.6, bf16[1024,8192]{1,0:T(8,128)(2,1)} %param.7, bf16[1024,64]{0,1:T(8,128)(2,1)S(1)} %copy-done.2, pred[]{:T(512)S(6)} %eq.18, pred[]{:T(512)S(6)} %gt.11), kind=kOutput, calls=%fused_computation.13 | convolution fusion | flops 537329664 | bytes 9568258 | tf_op jit(solution)/shard_map/dot_general | solution.py:28
  252.3 28.8 %all-reduce.7 = bf16[2048,64]{0,1:T(8,128)(2,1)S(1)} all-reduce(f32[2048,64]{0,1:T(8,128)S(1)} %fusion.9), channel_id=1, replica_groups=mesh['blk'=8,'slab'=4] {'blk'}, use_global_device_ids=true, to_apply=%region_4.5 | all-reduce | flops 131072 | bytes 786432 | tf_op jit(solution)/shard_map/psum | solution.py:30
  281.0 0.7 fusion.49
Async XLA Ops:
  6.5 38.4 %all-gather.2.cloned.1.call-start = ((), (), s32[]{:S(2)}) async-start(), calls=%async_computation.2 | async-start | bytes 1966080 | tf_op jit(solution)/shard_map/all_gather | solution.py:18
  7.3 138.0 %reduce-scatter.2.cloned.1.call-start = ((), (), s32[]{:S(2)}) async-start(), calls=%async_computation.3 | async-start | bytes 2359296 | tf_op jit(solution)/shard_map/reduce_scatter | solution.py:23
  102.2 43.1 %copy-start.2 = (bf16[1024,64]{0,1:T(8,128)(2,1)S(1)}, bf16[1024,64]{0,1:T(8,128)(2,1)}, u32[]{:S(2)}) copy-start(bf16[1024,64]{0,1:T(8,128)(2,1)} %param.9) | copy-start | bytes 393220
  145.3 32.7 %copy-start.3 = (f32[1024,64]{0,1:T(8,128)S(1)}, f32[1024,64]{0,1:T(8,128)}, u32[]{:S(2)}) copy-start(f32[1024,64]{0,1:T(8,128)} %reduce-scatter.2.cloned.1.call-done) | copy-start | bytes 786436
  178.0 3.7 %copy-start = (bf16[2048,1024]{1,0:T(8,128)(2,1)S(1)}, bf16[2048,1024]{1,0:T(8,128)(2,1)}, u32[]{:S(2)}) copy-start(bf16[2048,1024]{1,0:T(8,128)(2,1)} %param.8) | copy-start | bytes 12582916
  212.2 3.8 %copy-start.1 = (bf16[2048,1024]{1,0:T(8,128)(2,1)S(1)}, bf16[2048,1024]{1,0:T(8,128)(2,1)}, u32[]{:S(2)}) copy-start(bf16[2048,1024]{1,0:T(8,128)(2,1)} %param.8) | copy-start | bytes 12582916
Sparse Core Ops, SparseCore 0:
  8.9 35.9 all-gather.1
  103.9 41.3 reduce-scatter.1
where the time goes:
time: 293 us; the launch traced here: 289 us
  blocking collectives  166 us (57%)
  waiting for transfers between devices  79.8 us (27%)
  matrix products  27 us (9%)
  between operations  13.5 us (5%)
    psum x4, blocking collectives, body(): newest = lax.psum(term, 'blk').astype(jnp.bfloat16)  116 us
    all_to_all x1, blocking collectives, body(): lax.all_to_all(partial_value, 'slab', split_axis=1, concat_axis=0, tiled=...  50.4 us
    reduce_scatter x1, waiting for transfers between devices, body(): lax.psum_scatter(window_terms, 'blk', scatter_dimension=0, tiled=True)  41.5 us
    all_gather x1, waiting for transfers between devices, body(): lax.all_gather(solved, 'slab', axis=1, tiled=True)  37.6 us
    dot_general x4, matrix products, body(): term = jnp.dot(inv_diag, resid, preferred_element_type=jnp.float32)  12.6 us
    dot_general x2, matrix products, body(): update = jnp.dot(columns, newest, preferred_element_type=jnp.float32)  7.47 us
    dot_general x1, matrix products, body(): jnp.dot(old_factor, lax.all_gather(solved, 'slab', axis=1, tiled=True), p...  6.89 us
  transfers between devices with their start and end apart: 2, of which 2 were waited for; matrix products, arithmetic and copies ran while one was open for 0% of the time, Pallas kernels for 0%

commit v1 on v0

v1 whole, which is shorter than its diff:
```python
import functools

import jax
import jax.numpy as jnp
from jax import lax
from jax.experimental import pallas as pl
from jax.experimental.pallas import tpu as pltpu
from jax.sharding import PartitionSpec as P

STEPS = 4
CHUNKS = 2
MESH = pl.DeviceIdType.MESH
F32 = jnp.float32
BF16 = jnp.bfloat16


def swap_halves(value):
    return pltpu.roll(value, value.shape[1] // 2, 1)


def left_half(shape):
    return lax.broadcasted_iota(jnp.int32, shape, 1) < shape[1] // 2


def pack(upper, lower):
    return jnp.where(left_half(upper.shape), upper, swap_halves(lower))


def product(matrix_ref, rows, packed):
    half = packed.shape[0]
    first = jnp.dot(matrix_ref[rows, :half], packed, preferred_element_type=F32)
    second = jnp.dot(matrix_ref[rows, half:], packed, preferred_element_type=F32)
    return first + swap_halves(second)


def kernel(
    n_blk,
    n_slab,
    factor_hbm,
    solved_ref,
    band_hbm,
    inv_hbm,
    rhs_ref,
    out_ref,
    factor,
    band,
    inv,
    shards,
    parts,
    arrived,
    reduced,
    earlier,
    accum,
    resid,
    newest,
    factor_sem,
    band_sem,
    inv_sem,
    inv_send,
    shard_recv,
    up_send,
    down_send,
    part_send,
    part_recv,
    red_send,
    red_recv,
    resid_send,
    resid_recv,
    new_send,
    new_recv,
    fwd_send,
):
    b = lax.axis_index("blk")
    s = lax.axis_index("slab")
    width = rhs_ref.shape[1]
    own_rows = rhs_ref.shape[0]
    block_rows = inv_hbm.shape[0]
    group = block_rows // own_rows
    own_block = b // group
    member = b % group
    window = factor_hbm.shape[0]
    piece = shards.shape[1] // CHUNKS
    half = parts.shape[2]
    per_owner = own_rows // (2 * half)
    owners = window // own_rows
    tiles = factor_sem.shape[0]
    tile = window // tiles

    def remote(src, dst, send, recv, blk, slab):
        return pltpu.make_async_remote_copy(
            src_ref=src, dst_ref=dst, send_sem=send, recv_sem=recv,
            device_id=(blk, slab), device_id_type=MESH,
        )

    depth = solved_ref.shape[0]
    upper = solved_ref[: depth // 2, :].astype(F32)
    lower = solved_ref[depth // 2 :, :].astype(F32)
    shards[s] = jnp.concatenate([upper, lower], axis=1).astype(BF16)

    def shard_copy(which, chunk, up):
        ref = shards.at[which, pl.ds(chunk * piece, piece)]
        send = up_send if up else down_send
        return remote(ref, ref, send.at[which, chunk], shard_recv.at[which, chunk], b, s + 1 if up else s - 1)

    def pass_on(which, chunk, up):
        @pl.when(s < n_slab - 1 if up else s > 0)
        def _():
            shard_copy(which, chunk, up).start()

    for chunk in range(CHUNKS):
        pass_on(s, chunk, True)
        pass_on(s, chunk, False)

    def factor_copy(t):
        rows = pl.ds(t * tile, tile)
        return pltpu.make_async_copy(factor_hbm.at[rows], factor.at[rows], factor_sem.at[t])

    for t in range(tiles):
        factor_copy(t).start()

    def inv_remote(peer):
        return remote(
            inv_hbm.at[pl.ds(peer * own_rows, own_rows)], inv.at[member],
            inv_send.at[peer], inv_sem.at[member], own_block * group + peer, s,
        )

    inv_own = pltpu.make_async_copy(
        inv_hbm.at[pl.ds(member * own_rows, own_rows)], inv.at[member], inv_sem.at[member]
    )
    inv_own.start()
    for d in range(1, group):
        inv_remote((member + d) % group).start()

    def band_copy(k, m):
        return pltpu.make_async_copy(
            band_hbm.at[:, pl.ds(k * block_rows + m * own_rows, own_rows)], band.at[k, m], band_sem.at[k, m]
        )

    for k in range(STEPS - 1):
        @pl.when(own_block > k)
        def _():
            for m in range(group):
                band_copy(k, m).start()

    def part_copy(which, d):
        c = (b + d) % n_blk
        return remote(
            parts.at[which, c], arrived.at[which, n_blk - d - 1],
            part_send.at[which], part_recv.at[which], c, s,
        )

    def multiply(which, first_time):
        def step(t, carry):
            if first_time:
                factor_copy(t).wait()
            rows = pl.ds(t * tile, tile)
            value = product(factor, rows, shards[which])
            for i in range(tile // (2 * half)):
                base = i * 2 * half
                packed = pack(value[base : base + half], value[base + half : base + 2 * half])
                parts[which, t * (tile // (2 * half)) + i] = packed.astype(BF16)
            return carry

        lax.fori_loop(0, tiles, step, 0)
        lax.fori_loop(1, n_blk, lambda d, carry: (part_copy(which, d).start(), carry)[1], 0)

    def red_remote(which):
        return remote(
            reduced.at[which], earlier.at[b % per_owner],
            red_send.at[which], red_recv.at[b % per_owner], s * owners + b // per_owner, which,
        )

    def red_local(which):
        return pltpu.make_async_copy(reduced.at[which], earlier.at[b % per_owner], red_recv.at[b % per_owner])

    def is_self(which):
        return jnp.logical_and(which == s, b == s * owners + b // per_owner)

    def all_parts(which):
        return pltpu.make_async_copy(arrived.at[which], arrived.at[which], part_recv.at[which])

    def combine(which):
        all_parts(which).wait()
        total = parts[which, b].astype(F32)
        for d in range(n_blk - 1):
            total = total + arrived[which, d].astype(F32)
        reduced[which] = total

        @pl.when(is_self(which))
        def _():
            red_local(which).start()

        @pl.when(jnp.logical_not(is_self(which)))
        def _():
            red_remote(which).start()

    def take(which, up):
        for chunk in range(CHUNKS):
            ref = shards.at[which, pl.ds(chunk * piece, piece)]
            remote(ref, ref, up_send.at[which, chunk], shard_recv.at[which, chunk], b, s).wait_recv()
            pass_on(which, chunk, up)

    def at_distance(t, action):
        if t == 0:
            action(s, None)
            return

        @pl.when(s >= t)
        def _():
            action(s - t, True)

        @pl.when(s + t < n_slab)
        def _():
            action(s + t, False)

    multiply(s, True)
    for t in range(1, n_slab):
        at_distance(t, take)
        at_distance(t, lambda which, up: multiply(which, False))
        at_distance(t - 1, lambda which, up: combine(which))
    at_distance(n_slab - 1, lambda which, up: combine(which))

    accum[:, :width] = rhs_ref[...].astype(F32)
    for i in range(per_owner):
        pltpu.make_async_copy(reduced.at[0], earlier.at[i], red_recv.at[i]).wait()
        base = i * 2 * half
        value = earlier[i]
        accum[base : base + half, :width] = accum[base : base + half, :width] - value[:, :width]
        low = swap_halves(value)
        accum[base + half : base + 2 * half, :width] = accum[base + half : base + 2 * half, :width] - low[:, :width]

    top = own_rows // 2
    row_tiles = max(1, own_rows // 256)
    row_tile = own_rows // row_tiles

    def resid_copy(peer):
        ref = resid.at[member]
        return remote(ref, ref, resid_send.at[peer], resid_recv.at[member], own_block * group + peer, s)

    def new_copy(k, j):
        ref = newest.at[k, member]
        return remote(ref, ref, new_send.at[k, j], new_recv.at[k, member], j * group + member, s)

    def forward_copy(k, peer):
        ref = newest.at[k, member]
        return remote(ref, ref, fwd_send.at[k, peer], new_recv.at[k, member], own_block * group + peer, s)

    def add_product(matrix_ref, packed, sign, fresh):
        def step(t, carry):
            rows = pl.ds(t * row_tile, row_tile)
            value = product(matrix_ref, rows, packed)
            if fresh:
                accum[rows, :] = value
            else:
                accum[rows, :] = accum[rows, :] + sign * value
            return carry

        lax.fori_loop(0, row_tiles, step, 0)

    for k in range(STEPS):
        @pl.when(own_block == k)
        def _():
            resid[member] = pack(accum[:top, :], accum[top:, :]).astype(BF16)
            for d in range(1, group):
                resid_copy((member + d) % group).start()
            inv_own.wait()
            add_product(inv.at[member], resid[member], 1.0, True)
            for d in range(1, group):
                peer = (member + d) % group
                pltpu.make_async_copy(inv_hbm.at[pl.ds(0, own_rows)], inv.at[peer], inv_sem.at[peer]).wait()
                pltpu.make_async_copy(resid.at[peer], resid.at[peer], resid_recv.at[peer]).wait()
                add_product(inv.at[peer], resid[peer], 1.0, False)
            if k + 1 < STEPS:
                newest[k, member] = pack(accum[:top, :], accum[top:, :]).astype(BF16)
                for j in range(k + 1, STEPS):
                    new_copy(k, j).start()
            out_ref[...] = accum[:, :width].astype(BF16)

        if k + 1 < STEPS:
            @pl.when(own_block > k)
            def _():
                ref = newest.at[k, member]
                pltpu.make_async_copy(ref, ref, new_recv.at[k, member]).wait()
                for d in range(1, group):
                    forward_copy(k, (member + d) % group).start()
                for m in range(group):
                    band_copy(k, m).wait()
                add_product(band.at[k, member], newest[k, member], -1.0, False)
                for d in range(1, group):
                    peer = (member + d) % group
                    ref = newest.at[k, peer]
                    pltpu.make_async_copy(ref, ref, new_recv.at[k, peer]).wait()
                    add_product(band.at[k, peer], newest[k, peer], -1.0, False)

    def sent(which, up):
        for chunk in range(CHUNKS):
            for way in (True, False):
                if up is None or up == way:
                    @pl.when(s < n_slab - 1 if way else s > 0)
                    def _():
                        shard_copy(which, chunk, way).wait_send()
        pltpu.make_async_copy(arrived.at[which], arrived.at[which], part_send.at[which]).wait()

        @pl.when(jnp.logical_not(is_self(which)))
        def _():
            red_remote(which).wait_send()

    for t in range(n_slab):
        at_distance(t, sent)
    for d in range(1, group):
        peer = (member + d) % group
        inv_remote(peer).wait_send()
        resid_copy(peer).wait_send()
    for k in range(STEPS - 1):
        @pl.when(own_block == k)
        def _():
            for j in range(k + 1, STEPS):
                new_copy(k, j).wait_send()

        @pl.when(own_block > k)
        def _():
            for d in range(1, group):
                forward_copy(k, (member + d) % group).wait_send()


def body(n_blk, n_slab, old_factor, solved, band, inv_diag, rhs):
    window, depth = old_factor.shape
    own_rows, width = rhs.shape
    block_rows = inv_diag.shape[0]
    group = block_rows // own_rows
    half = window // n_blk // 2
    per_owner = own_rows // (2 * half)
    lanes = 2 * width
    tiles = 4
    dma = pltpu.SemaphoreType.DMA
    vmem = pl.BlockSpec(memory_space=pltpu.VMEM)
    hbm = pl.BlockSpec(memory_space=pl.ANY)
    return pl.pallas_call(
        functools.partial(kernel, n_blk, n_slab),
        out_shape=jax.ShapeDtypeStruct(rhs.shape, BF16),
        in_specs=[hbm, vmem, hbm, hbm, vmem],
        out_specs=vmem,
        scratch_shapes=[
            pltpu.VMEM((window, depth), BF16),
            pltpu.VMEM((STEPS - 1, group, own_rows, own_rows), BF16),
            pltpu.VMEM((group, own_rows, own_rows), BF16),
            pltpu.VMEM((n_slab, depth // 2, lanes), BF16),
            pltpu.VMEM((n_slab, n_blk, half, lanes), BF16),
            pltpu.VMEM((n_slab, n_blk - 1, half, lanes), BF16),
            pltpu.VMEM((n_slab, half, lanes), F32),
            pltpu.VMEM((per_owner, half, lanes), F32),
            pltpu.VMEM((own_rows, lanes), F32),
            pltpu.VMEM((group, own_rows // 2, lanes), BF16),
            pltpu.VMEM((STEPS - 1, group, own_rows // 2, lanes), BF16),
            dma((tiles,)),
            dma((STEPS - 1, group)),
            dma((group,)),
            dma((group,)),
            dma((n_slab, CHUNKS)),
            dma((n_slab, CHUNKS)),
            dma((n_slab, CHUNKS)),
            dma((n_slab,)),
            dma((n_slab,)),
            dma((n_slab,)),
            dma((per_owner,)),
            dma((group,)),
            dma((group,)),
            dma((STEPS - 1, STEPS)),
            dma((STEPS - 1, group)),
            dma((STEPS - 1, group)),
        ],
        compiler_params=pltpu.CompilerParams(has_side_effects=True, vmem_limit_bytes=60 * 1024 * 1024),
        name="forward_window",
    )(old_factor, solved, band, inv_diag, rhs)


def solution(mesh):
    return jax.shard_map(
        functools.partial(body, mesh.shape["blk"], mesh.shape["slab"]),
        mesh=mesh,
        in_specs=(
            P("slab", "blk"),
            P("blk", "slab"),
            P("blk", None),
            P(None, "blk"),
            P("blk", "slab"),
        ),
        out_specs=P("blk", "slab"),
        check_vma=False,
    )
```

time: 293 us -> 91.2 us (0.31); the launches traced: 289 us -> 91 us
  blocking collectives: 166 us -> 0 us
  Pallas kernels: 0 us -> 85.4 us
  waiting for transfers between devices: 79.8 us -> 0 us
  matrix products: 27 us -> 0 us
  between operations: 13.5 us -> 0.01 us
  local copies, waits for them, and re-layouts: 1.51 us -> 5.63 us
    psum x4 -> x0, blocking collectives: 116 us -> none  [body(): newest = lax.psum(term, 'blk').astype(jnp.bfloat16)]
    pallas_call x0 -> x1, Pallas kernels: none -> 85.4 us  [body(): pl.pallas_call(functools.partial(kernel, n_blk, n_slab), out_shape=jax.Sh...]
    all_to_all x1 -> x0, blocking collectives: 50.4 us -> none  [body(): lax.all_to_all(partial_value, 'slab', split_axis=1, concat_axis=0, tiled=...]
    reduce_scatter x1 -> x0, waiting for transfers between devices: 41.5 us -> none  [body(): lax.psum_scatter(window_terms, 'blk', scatter_dimension=0, tiled=True)]
    all_gather x1 -> x0, waiting for transfers between devices: 37.6 us -> none  [body(): lax.all_gather(solved, 'slab', axis=1, tiled=True)]
    dot_general x7 -> x0, matrix products: 27 us -> none  [the longest x4 12.6 us: body(): term = jnp.dot(inv_diag, resid, preferred_element_type=jnp.float32)]
    unnamed x8 -> x2, local copies, waits for them, and re-layouts: 0.02 us -> 3.9 us
  transfers between devices with their start and end apart: 2 -> 0, of which waited for: 2 -> 0; matrix products, arithmetic and copies ran while one was open for 0% -> 0% of each run, Pallas kernels for 0% -> 0%
where the time goes in v1:
time: 91.2 us; the launch traced here: 91 us
  Pallas kernels  85.4 us (94%)
  local copies, waits for them, and re-layouts  5.63 us (6%)
    pallas_call x1, Pallas kernels, body(): pl.pallas_call(functools.partial(kernel, n_blk, n_slab), out_shape=jax.Sh...  85.4 us
    unnamed x2, local copies, waits for them, and re-layouts  3.9 us

profile of v1, /device:TPU:31, one launch (start us, length us, event | category | flops | bytes accessed | tf_op | source)
XLA Modules:
  0.0 91.0 jit_solution(6451549088935672322)
XLA Ops:
  0.0 1.8 %copy.7.rhs_ref = bf16[1024,64]{1,0:T(8,128)(2,1)} copy(bf16[1024,64]{0,1:T(8,128)(2,1)} %param.9) | data formatting | bytes 262144 | tf_op args[4]
  1.8 2.1 %copy.6.solved_ref = bf16[3072,64]{1,0:T(8,128)(2,1)} copy(bf16[3072,64]{0,1:T(8,128)(2,1)} %param.6) | data formatting | bytes 786432 | tf_op args[1]
  3.9 85.4 %forward_window.1 = bf16[1024,64]{1,0:T(8,128)(2,1)} custom-call(bf16[2048,3072]{1,0:T(8,128)(2,1)} %factor_hbm.1, bf16[3072,64]{1,0:T(8,128)(2,1)} %copy.6.solved_ref, bf16[1024,8192]{1,0:T(8,128)(2,1)} %band_hbm.1, bf16[2048,1024]{1,0:T(8,128)(2,1)} %inv_hbm.1, bf16[1024,64]{1,0:T(8,128)(2,1)} %copy.7.rhs_ref), custom_call_target="tpu_custom_call" | custom-call | tf_op jit(solution)/shard_map/forward_window/pallas_call | solution.py:338
  89.3 1.7 %copy.8 = bf16[1024,64]{0,1:T(8,128)(2,1)} copy(bf16[1024,64]{1,0:T(8,128)(2,1)} %forward_window.1) | data formatting | bytes 262144 | tf_op jit(solution)/shard_map/forward_window/pallas_call | solution.py:338

commit v2 on v1

--- a/solution.py
+++ b/solution.py
@@ -37,7 +37,7 @@
     n_blk,
     n_slab,
     factor_hbm,
-    solved_ref,
+    solved_hbm,
     band_hbm,
     inv_hbm,
     rhs_ref,
@@ -46,6 +46,8 @@
     band,
     inv,
     shards,
+    columns,
+    partial,
     parts,
     arrived,
     reduced,
@@ -72,14 +74,13 @@
 ):
     b = lax.axis_index("blk")
     s = lax.axis_index("slab")
-    width = rhs_ref.shape[1]
-    own_rows = rhs_ref.shape[0]
+    width, own_rows = rhs_ref.shape
     block_rows = inv_hbm.shape[0]
     group = block_rows // own_rows
     own_block = b // group
     member = b % group
     window = factor_hbm.shape[0]
-    piece = shards.shape[1] // CHUNKS
+    piece = shards.shape[3]
     half = parts.shape[2]
     per_owner = own_rows // (2 * half)
     owners = window // own_rows
@@ -92,24 +93,26 @@
             device_id=(blk, slab), device_id_type=MESH,
         )
 
-    depth = solved_ref.shape[0]
-    upper = solved_ref[: depth // 2, :].astype(F32)
-    lower = solved_ref[depth // 2 :, :].astype(F32)
-    shards[s] = jnp.concatenate([upper, lower], axis=1).astype(BF16)
-
-    def shard_copy(which, chunk, up):
-        ref = shards.at[which, pl.ds(chunk * piece, piece)]
+    def shard_copy(which, chunk, up, own):
+        ref = shards.at[which, chunk]
+        source = solved_hbm.at[:, pl.ds(chunk * piece, piece)] if own else ref
         send = up_send if up else down_send
-        return remote(ref, ref, send.at[which, chunk], shard_recv.at[which, chunk], b, s + 1 if up else s - 1)
-
-    def pass_on(which, chunk, up):
+        return remote(source, ref, send.at[which, chunk], shard_recv.at[which, chunk], b, s + 1 if up else s - 1)
+
+    def pass_on(which, chunk, up, own=False):
         @pl.when(s < n_slab - 1 if up else s > 0)
         def _():
-            shard_copy(which, chunk, up).start()
+            shard_copy(which, chunk, up, own).start()
+
+    def own_copy(chunk):
+        return pltpu.make_async_copy(
+            solved_hbm.at[:, pl.ds(chunk * piece, piece)], shards.at[s, chunk], shard_recv.at[s, chunk]
+        )
 
     for chunk in range(CHUNKS):
-        pass_on(s, chunk, True)
-        pass_on(s, chunk, False)
+        pass_on(s, chunk, True, True)
+        pass_on(s, chunk, False, True)
+        own_copy(chunk).start()
 
     def factor_copy(t):
         rows = pl.ds(t * tile, tile)
@@ -142,27 +145,41 @@
             for m in range(group):
                 band_copy(k, m).start()
 
-    def part_copy(which, d):
-        c = (b + d) % n_blk
+    def part_copy(which, c):
         return remote(
-            parts.at[which, c], arrived.at[which, n_blk - d - 1],
+            parts.at[which, c], arrived.at[which, lax.rem(b - c + n_blk, n_blk) - 1],
             part_send.at[which], part_recv.at[which], c, s,
         )
 
-    def multiply(which, first_time):
-        def step(t, carry):
-            if first_time:
+    def multiply(which, chunk, first_time, side):
+        columns[...] = jnp.swapaxes(shards[which, chunk].astype(F32), 0, 1).astype(BF16)
+        span = slice(chunk * piece, (chunk + 1) * piece)
+        per_tile = tile // (2 * half)
+
+        def step(i, carry):
+            t = lax.rem(i + lax.div(b * tiles, n_blk), tiles)
+            if first_time and chunk == 0:
                 factor_copy(t).wait()
             rows = pl.ds(t * tile, tile)
-            value = product(factor, rows, shards[which])
-            for i in range(tile // (2 * half)):
+            value = jnp.dot(factor[rows, span], columns[...], preferred_element_type=F32)
+            if chunk > 0:
+                value = partial[side, rows, :] + value
+            if chunk < CHUNKS - 1:
+                partial[side, rows, :] = value
+                return carry
+            for i in range(per_tile):
                 base = i * 2 * half
-                packed = pack(value[base : base + half], value[base + half : base + 2 * half])
-                parts[which, t * (tile // (2 * half)) + i] = packed.astype(BF16)
+                c = t * per_tile + i
+                packed = jnp.concatenate([value[base : base + half], value[base + half : base + 2 * half]], axis=1)
+                parts[which, c] = packed.astype(BF16)
+
+                @pl.when(c != b)
+                def _():
+                    part_copy(which, c).start()
+
             return carry
 
         lax.fori_loop(0, tiles, step, 0)
-        lax.fori_loop(1, n_blk, lambda d, carry: (part_copy(which, d).start(), carry)[1], 0)
 
     def red_remote(which):
         return remote(
@@ -194,11 +211,10 @@
         def _():
             red_remote(which).start()
 
-    def take(which, up):
-        for chunk in range(CHUNKS):
-            ref = shards.at[which, pl.ds(chunk * piece, piece)]
-            remote(ref, ref, up_send.at[which, chunk], shard_recv.at[which, chunk], b, s).wait_recv()
-            pass_on(which, chunk, up)
+    def take(which, chunk, up):
+        ref = shards.at[which, chunk]
+        remote(ref, ref, up_send.at[which, chunk], shard_recv.at[which, chunk], b, s).wait_recv()
+        pass_on(which, chunk, up)
 
     def at_distance(t, action):
         if t == 0:
@@ -213,14 +229,17 @@
         def _():
             action(s + t, False)
 
-    multiply(s, True)
+    for chunk in range(CHUNKS):
+        own_copy(chunk).wait()
+        multiply(s, chunk, True, 0)
     for t in range(1, n_slab):
-        at_distance(t, take)
-        at_distance(t, lambda which, up: multiply(which, False))
+        for chunk in range(CHUNKS):
+            at_distance(t, lambda which, up: take(which, chunk, up))
+            at_distance(t, lambda which, up: multiply(which, chunk, False, 0 if up else 1))
         at_distance(t - 1, lambda which, up: combine(which))
     at_distance(n_slab - 1, lambda which, up: combine(which))
 
-    accum[:, :width] = rhs_ref[...].astype(F32)
+    accum[:, :width] = jnp.swapaxes(rhs_ref[...].astype(F32), 0, 1)
     for i in range(per_owner):
         pltpu.make_async_copy(reduced.at[0], earlier.at[i], red_recv.at[i]).wait()
         base = i * 2 * half
@@ -274,7 +293,7 @@
                 newest[k, member] = pack(accum[:top, :], accum[top:, :]).astype(BF16)
                 for j in range(k + 1, STEPS):
                     new_copy(k, j).start()
-            out_ref[...] = accum[:, :width].astype(BF16)
+            out_ref[...] = jnp.swapaxes(accum[:, :width], 0, 1).astype(BF16)
 
         if k + 1 < STEPS:
             @pl.when(own_block > k)
@@ -298,7 +317,7 @@
                 if up is None or up == way:
                     @pl.when(s < n_slab - 1 if way else s > 0)
                     def _():
-                        shard_copy(which, chunk, way).wait_send()
+                        shard_copy(which, chunk, way, False).wait_send()
         pltpu.make_async_copy(arrived.at[which], arrived.at[which], part_send.at[which]).wait()
 
         @pl.when(jnp.logical_not(is_self(which)))
@@ -337,14 +356,16 @@
     hbm = pl.BlockSpec(memory_space=pl.ANY)
     return pl.pallas_call(
         functools.partial(kernel, n_blk, n_slab),
-        out_shape=jax.ShapeDtypeStruct(rhs.shape, BF16),
-        in_specs=[hbm, vmem, hbm, hbm, vmem],
+        out_shape=jax.ShapeDtypeStruct((width, own_rows), BF16),
+        in_specs=[hbm, hbm, hbm, hbm, vmem],
         out_specs=vmem,
         scratch_shapes=[
             pltpu.VMEM((window, depth), BF16),
             pltpu.VMEM((STEPS - 1, group, own_rows, own_rows), BF16),
             pltpu.VMEM((group, own_rows, own_rows), BF16),
-            pltpu.VMEM((n_slab, depth // 2, lanes), BF16),
+            pltpu.VMEM((n_slab, CHUNKS, width, depth // CHUNKS), BF16),
+            pltpu.VMEM((depth // CHUNKS, width), BF16),
+            pltpu.VMEM((2, window, width), F32),
             pltpu.VMEM((n_slab, n_blk, half, lanes), BF16),
             pltpu.VMEM((n_slab, n_blk - 1, half, lanes), BF16),
             pltpu.VMEM((n_slab, half, lanes), F32),
@@ -371,7 +392,7 @@
         ],
         compiler_params=pltpu.CompilerParams(has_side_effects=True, vmem_limit_bytes=60 * 1024 * 1024),
         name="forward_window",
-    )(old_factor, solved, band, inv_diag, rhs)
+    )(old_factor, solved.T, band, inv_diag, rhs.T).T
 
 
 def solution(mesh):

time: 91.2 us -> 84 us (0.921)
  local copies, waits for them, and re-layouts: 5.63 us -> 1.57 us
  Pallas kernels: 85.4 us -> 82.2 us
    pallas_call x1, Pallas kernels: 85.4 us -> 82.2 us  [body(): pl.pallas_call(functools.partial(kernel, n_blk, n_slab), out_shape=jax.Sh...]
    unnamed x2 -> x1, local copies, waits for them, and re-layouts: 3.9 us -> 1.57 us
    pallas_call x1 -> x0, local copies, waits for them, and re-layouts: 1.73 us -> none  [body(): pl.pallas_call(functools.partial(kernel, n_blk, n_slab), out_shape=jax.Sh...]
where the time goes in v2:
time: 84 us; the launch traced here: 83.8 us
  Pallas kernels  82.2 us (98%)
  local copies, waits for them, and re-layouts  1.57 us (2%)
    pallas_call x1, Pallas kernels, body(): pl.pallas_call(functools.partial(kernel, n_blk, n_slab), out_shape=jax.Sh...  82.2 us

profile of v2, /device:TPU:31, one launch (start us, length us, event | category | flops | bytes accessed | tf_op | source)
XLA Modules:
  0.0 83.8 jit_solution(75624646261295281)
XLA Ops:
  0.0 82.2 %forward_window.1 = bf16[64,1024]{1,0:T(8,128)(2,1)} custom-call(bf16[2048,3072]{1,0:T(8,128)(2,1)} %factor_hbm.1, bf16[64,3072]{1,0:T(8,128)(2,1)} %bitcast.4, bf16[1024,8192]{1,0:T(8,128)(2,1)} %band_hbm.1, bf16[2048,1024]{1,0:T(8,128)(2,1)} %inv_hbm.1, bf16[64,1024]{1,0:T(8,128)(2,1)} %bitcast.5), custom_call_target="tpu_custom_call" | custom-call | tf_op jit(solution)/shard_map/forward_window/pallas_call | solution.py:357
  82.2 1.6 %copy.7 = bf16[1024,64]{0,1:T(8,128)(2,1)} copy(bf16[1024,64]{0,1:T(8,128)(2,1)} %bitcast.3) | data formatting | bytes 262144

commit v3 on v2

--- a/solution.py
+++ b/solution.py
@@ -93,6 +93,23 @@
             device_id=(blk, slab), device_id_type=MESH,
         )
 
+    barrier = pltpu.get_barrier_semaphore()
+
+    def greet(blk, slab):
+        pl.semaphore_signal(barrier, inc=1, device_id=(blk, slab), device_id_type=MESH)
+
+    @pl.when(s > 0)
+    def _():
+        greet(b, s - 1)
+
+    @pl.when(s < n_slab - 1)
+    def _():
+        greet(b, s + 1)
+
+    for d in range(1, n_blk):
+        greet(lax.rem(b + d, n_blk), s)
+    pl.semaphore_wait(barrier, n_blk - 1 + (s > 0).astype(jnp.int32) + (s < n_slab - 1).astype(jnp.int32))
+
     def shard_copy(which, chunk, up, own):
         ref = shards.at[which, chunk]
         source = solved_hbm.at[:, pl.ds(chunk * piece, piece)] if own else ref
@@ -390,7 +407,7 @@
             dma((STEPS - 1, group)),
             dma((STEPS - 1, group)),
         ],
-        compiler_params=pltpu.CompilerParams(has_side_effects=True, vmem_limit_bytes=60 * 1024 * 1024),
+        compiler_params=pltpu.CompilerParams(collective_id=0, has_side_effects=True, vmem_limit_bytes=60 * 1024 * 1024),
         name="forward_window",
     )(old_factor, solved.T, band, inv_diag, rhs.T).T
 

time: 84 us -> 79.7 us (0.949)
  Pallas kernels: 82.2 us -> 77.9 us
    pallas_call x1, Pallas kernels: 82.2 us -> 77.9 us  [body(): pl.pallas_call(functools.partial(kernel, n_blk, n_slab), out_shape=jax.Sh...]
where the time goes in v3:
time: 79.7 us; the launch traced here: 79.5 us
  Pallas kernels  77.9 us (98%)
  local copies, waits for them, and re-layouts  1.57 us (2%)
    pallas_call x1, Pallas kernels, body(): pl.pallas_call(functools.partial(kernel, n_blk, n_slab), out_shape=jax.Sh...  77.9 us

profile of v3, /device:TPU:31, one launch (start us, length us, event | category | flops | bytes accessed | tf_op | source)
XLA Modules:
  0.0 79.5 jit_solution(3474731515229121117)
XLA Ops:
  0.0 77.9 %forward_window.1 = bf16[64,1024]{1,0:T(8,128)(2,1)} custom-call(bf16[2048,3072]{1,0:T(8,128)(2,1)} %factor_hbm.1, bf16[64,3072]{1,0:T(8,128)(2,1)} %bitcast.4, bf16[1024,8192]{1,0:T(8,128)(2,1)} %band_hbm.1, bf16[2048,1024]{1,0:T(8,128)(2,1)} %inv_hbm.1, bf16[64,1024]{1,0:T(8,128)(2,1)} %bitcast.5), custom_call_target="tpu_custom_call" | custom-call | tf_op jit(solution)/shard_map/forward_window/pallas_call | solution.py:374
  78.0 1.6 %copy.7 = bf16[1024,64]{0,1:T(8,128)(2,1)} copy(bf16[1024,64]{0,1:T(8,128)(2,1)} %bitcast.3) | data formatting | bytes 262144

commit v4 on v3

--- a/solution.py
+++ b/solution.py
@@ -26,10 +26,12 @@
     return jnp.where(left_half(upper.shape), upper, swap_halves(lower))
 
 
-def product(matrix_ref, rows, packed):
-    half = packed.shape[0]
-    first = jnp.dot(matrix_ref[rows, :half], packed, preferred_element_type=F32)
-    second = jnp.dot(matrix_ref[rows, half:], packed, preferred_element_type=F32)
+def product(matrix_ref, rows, packed, start, half):
+    count = packed.shape[0]
+    upper = matrix_ref[rows, start : start + count]
+    lower = matrix_ref[rows, half + start : half + start + count]
+    first = jnp.dot(upper, packed, preferred_element_type=F32)
+    second = jnp.dot(lower, packed, preferred_element_type=F32)
     return first + swap_halves(second)
 
 
@@ -266,25 +268,31 @@
         accum[base + half : base + 2 * half, :width] = accum[base + half : base + 2 * half, :width] - low[:, :width]
 
     top = own_rows // 2
-    row_tiles = max(1, own_rows // 256)
-    row_tile = own_rows // row_tiles
+    cuts = newest.shape[2]
+    cut = newest.shape[3]
+    row_tile = min(own_rows, 512)
+    row_tiles = own_rows // row_tile
 
     def resid_copy(peer):
         ref = resid.at[member]
         return remote(ref, ref, resid_send.at[peer], resid_recv.at[member], own_block * group + peer, s)
 
-    def new_copy(k, j):
-        ref = newest.at[k, member]
-        return remote(ref, ref, new_send.at[k, j], new_recv.at[k, member], j * group + member, s)
-
-    def forward_copy(k, peer):
-        ref = newest.at[k, member]
-        return remote(ref, ref, fwd_send.at[k, peer], new_recv.at[k, member], own_block * group + peer, s)
-
-    def add_product(matrix_ref, packed, sign, fresh):
+    def new_copy(k, j, i):
+        ref = newest.at[k, member, i]
+        return remote(ref, ref, new_send.at[k, j, i], new_recv.at[k, member, i], j * group + member, s)
+
+    def forward_copy(k, peer, i):
+        ref = newest.at[k, member, i]
+        return remote(ref, ref, fwd_send.at[k, peer, i], new_recv.at[k, member, i], own_block * group + peer, s)
+
+    def await_new(k, m, i):
+        ref = newest.at[k, m, i]
+        pltpu.make_async_copy(ref, ref, new_recv.at[k, m, i]).wait()
+
+    def add_product(matrix_ref, packed, start, sign, fresh):
         def step(t, carry):
             rows = pl.ds(t * row_tile, row_tile)
-            value = product(matrix_ref, rows, packed)
+            value = product(matrix_ref, rows, packed, start, top)
             if fresh:
                 accum[rows, :] = value
             else:
@@ -300,33 +308,41 @@
             for d in range(1, group):
                 resid_copy((member + d) % group).start()
             inv_own.wait()
-            add_product(inv.at[member], resid[member], 1.0, True)
+            add_product(inv.at[member], resid[member], 0, 1.0, True)
             for d in range(1, group):
                 peer = (member + d) % group
                 pltpu.make_async_copy(inv_hbm.at[pl.ds(0, own_rows)], inv.at[peer], inv_sem.at[peer]).wait()
                 pltpu.make_async_copy(resid.at[peer], resid.at[peer], resid_recv.at[peer]).wait()
-                add_product(inv.at[peer], resid[peer], 1.0, False)
-            if k + 1 < STEPS:
-                newest[k, member] = pack(accum[:top, :], accum[top:, :]).astype(BF16)
-                for j in range(k + 1, STEPS):
-                    new_copy(k, j).start()
+                if d < group - 1:
+                    add_product(inv.at[peer], resid[peer], 0, 1.0, False)
+            last = (member + group - 1) % group
+            for i in range(cuts):
+                upper = slice(i * cut, (i + 1) * cut)
+                lower = slice(top + i * cut, top + (i + 1) * cut)
+                for rows in (upper, lower):
+                    accum[rows, :] = accum[rows, :] + product(inv.at[last], rows, resid[last], 0, top)
+                if k + 1 < STEPS:
+                    newest[k, member, i] = pack(accum[upper, :], accum[lower, :]).astype(BF16)
+                    for j in range(k + 1, STEPS):
+                        new_copy(k, j, i).start()
             out_ref[...] = jnp.swapaxes(accum[:, :width], 0, 1).astype(BF16)
 
         if k + 1 < STEPS:
             @pl.when(own_block > k)
             def _():
-                ref = newest.at[k, member]
-                pltpu.make_async_copy(ref, ref, new_recv.at[k, member]).wait()
-                for d in range(1, group):
-                    forward_copy(k, (member + d) % group).start()
-                for m in range(group):
-                    band_copy(k, m).wait()
-                add_product(band.at[k, member], newest[k, member], -1.0, False)
+                for i in range(cuts):
+                    await_new(k, member, i)
+                    for d in range(1, group):
+                        forward_copy(k, (member + d) % group, i).start()
+                    if i == 0:
+                        for m in range(group):
+                            band_copy(k, m).wait()
+                    add_product(band.at[k, member], newest[k, member, i], i * cut, -1.0, False)
                 for d in range(1, group):
                     peer = (member + d) % group
-                    ref = newest.at[k, peer]
-                    pltpu.make_async_copy(ref, ref, new_recv.at[k, peer]).wait()
-                    add_product(band.at[k, peer], newest[k, peer], -1.0, False)
+                    for i in range(cuts):
+                        await_new(k, peer, i)
+                        add_product(band.at[k, peer], newest[k, peer, i], i * cut, -1.0, False)
 
     def sent(which, up):
         for chunk in range(CHUNKS):
@@ -351,12 +367,14 @@
         @pl.when(own_block == k)
         def _():
             for j in range(k + 1, STEPS):
-                new_copy(k, j).wait_send()
+                for i in range(cuts):
+                    new_copy(k, j, i).wait_send()
 
         @pl.when(own_block > k)
         def _():
             for d in range(1, group):
-                forward_copy(k, (member + d) % group).wait_send()
+                for i in range(cuts):
+                    forward_copy(k, (member + d) % group, i).wait_send()
 
 
 def body(n_blk, n_slab, old_factor, solved, band, inv_diag, rhs):
@@ -368,6 +386,7 @@
     per_owner = own_rows // (2 * half)
     lanes = 2 * width
     tiles = 4
+    cuts = 2 if own_rows >= 512 else 1
     dma = pltpu.SemaphoreType.DMA
     vmem = pl.BlockSpec(memory_space=pltpu.VMEM)
     hbm = pl.BlockSpec(memory_space=pl.ANY)
@@ -389,7 +408,7 @@
             pltpu.VMEM((per_owner, half, lanes), F32),
             pltpu.VMEM((own_rows, lanes), F32),
             pltpu.VMEM((group, own_rows // 2, lanes), BF16),
-            pltpu.VMEM((STEPS - 1, group, own_rows // 2, lanes), BF16),
+            pltpu.VMEM((STEPS - 1, group, cuts, own_rows // 2 // cuts, lanes), BF16),
             dma((tiles,)),
             dma((STEPS - 1, group)),
             dma((group,)),
@@ -403,9 +422,9 @@
             dma((per_owner,)),
             dma((group,)),
             dma((group,)),
-            dma((STEPS - 1, STEPS)),
-            dma((STEPS - 1, group)),
-            dma((STEPS - 1, group)),
+            dma((STEPS - 1, STEPS, cuts)),
+            dma((STEPS - 1, group, cuts)),
+            dma((STEPS - 1, group, cuts)),
         ],
         compiler_params=pltpu.CompilerParams(collective_id=0, has_side_effects=True, vmem_limit_bytes=60 * 1024 * 1024),
         name="forward_window",

time: 79.7 us -> 78.1 us (0.980)
  Pallas kernels: 77.9 us -> 76.4 us
    pallas_call x1, Pallas kernels: 77.9 us -> 76.4 us  [body(): pl.pallas_call(functools.partial(kernel, n_blk, n_slab), out_shape=jax.Sh...]
where the time goes in v4:
time: 78.1 us; the launch traced here: 78 us
  Pallas kernels  76.4 us (98%)
  local copies, waits for them, and re-layouts  1.57 us (2%)
    pallas_call x1, Pallas kernels, body(): pl.pallas_call(functools.partial(kernel, n_blk, n_slab), out_shape=jax.Sh...  76.4 us
    unnamed x1, local copies, waits for them, and re-layouts  1.57 us

profile of v4, /device:TPU:31, one launch (start us, length us, event | category | flops | bytes accessed | tf_op | source)
XLA Modules:
  0.0 78.0 jit_solution(15036445419643013130)
XLA Ops:
  0.0 76.4 %forward_window.1 = bf16[64,1024]{1,0:T(8,128)(2,1)} custom-call(bf16[2048,3072]{1,0:T(8,128)(2,1)} %factor_hbm.1, bf16[64,3072]{1,0:T(8,128)(2,1)} %bitcast.4, bf16[1024,8192]{1,0:T(8,128)(2,1)} %band_hbm.1, bf16[2048,1024]{1,0:T(8,128)(2,1)} %inv_hbm.1, bf16[64,1024]{1,0:T(8,128)(2,1)} %bitcast.5), custom_call_target="tpu_custom_call" | custom-call | tf_op jit(solution)/shard_map/forward_window/pallas_call | solution.py:393
  76.4 1.6 %copy.7 = bf16[1024,64]{0,1:T(8,128)(2,1)} copy(bf16[1024,64]{0,1:T(8,128)(2,1)} %bitcast.3) | data formatting | bytes 262144
